TPU v7x, 128 devices: a whole 4x4x4 slice. The times are simulated.
128 devices in a mesh: row: 8 (over x, z_lo), col: 16 (over y, z_hi, core).
Axes of the slice: x: 4, y: 4, z: 4 (z_hi: 2, z_lo: 2; z = z_hi * 2 + z_lo), core: 2. Of those that a mesh axis runs over, the one named last changes fastest.
Arguments:
- gate_pre: bfloat16 [2048, 26624], P('col', 'row'), may hold values from -6 to 6
- up_pre: bfloat16 [2048, 26624], P('col', 'row'), may hold values from -6 to 6
- residual: bfloat16 [2048, 16384], P('row', 'col'), may hold values from -6 to 6
- base_weight: bfloat16 [26624, 16384], P('row', 'col'), may hold values from -0.0390625 to 0.0390625
- perturb: bfloat16 [26624, 16384], P('row', 'col'), may hold values from -0.0390625 to 0.0390625
- exponents: int32 [208, 16384], P('row', 'col'), may hold values from -2 to 1
Outputs:
- plus_out: bfloat16 [2048, 16384], P('row', 'col')
- minus_out: bfloat16 [2048, 16384], P('row', 'col')
All inputs are finite; a program needn't handle non-finite values.
Results may differ from a plain program's by a relative error of at most 0.004.
Values may be sent and summed in bfloat16 or wider, within the bound.
A program may use at most 128 MiB of HBM per device.

v0:
```python
import jax
import jax.numpy as jnp
from jax import lax
from jax.sharding import Mesh
from jax.sharding import PartitionSpec as P

ROW = ("row_0", "row_1")
step_size = 0.25


def own_rows(so_far, axes):
    for axis in axes:
        so_far = lax.psum_scatter(so_far, axis, scatter_dimension=0, tiled=True)
    return so_far


def swiglu(gate_part, up_part):
    return (jax.nn.silu(gate_part.astype(jnp.float32)) * up_part.astype(jnp.float32)).astype(
        jnp.bfloat16
    )


def on_device(gate_pre, up_pre, residual, base_weight, perturb, exponents):
    hidden = lax.all_gather(swiglu(gate_pre, up_pre), "col", axis=0, tiled=True)
    group_size = base_weight.shape[0] // exponents.shape[0]
    factor = jnp.repeat(jnp.exp2(exponents.astype(jnp.float32)), group_size, axis=0)
    shift = step_size * factor * perturb.astype(jnp.float32)
    weight_full = base_weight.astype(jnp.float32)
    plus_weight = (weight_full + shift).astype(jnp.bfloat16)
    minus_weight = (weight_full - shift).astype(jnp.bfloat16)
    stream = residual.astype(jnp.float32)
    stacked = jnp.concatenate([plus_weight, minus_weight], axis=1)
    summed = own_rows(jnp.dot(hidden, stacked, preferred_element_type=jnp.float32), ROW)
    columns = base_weight.shape[1]
    plus_sum = summed[:, :columns]
    minus_sum = summed[:, columns:]
    plus_out = (stream + plus_sum).astype(jnp.bfloat16)
    minus_out = (stream + minus_sum).astype(jnp.bfloat16)
    return (plus_out, minus_out)


def solution(mesh):
    finer = Mesh(mesh.devices.reshape(4, 2, mesh.shape["col"]), ("row_0", "row_1", "col"))
    in_specs = (
        P("col", ROW),
        P("col", ROW),
        P(ROW, "col"),
        P(ROW, "col"),
        P(ROW, "col"),
        P(ROW, "col"),
    )
    out_specs = (P(ROW, "col"), P(ROW, "col"))
    return jax.shard_map(
        on_device, mesh=finer, in_specs=in_specs, out_specs=out_specs, check_vma=False
    )
```

profile of v0, /device:TPU:1, one launch (start us, length us, event | category | flops | bytes accessed | tf_op | source)
XLA Modules:
  0.0 360.9 jit_solution(1346917091632960387)
XLA Ops:
  7.2 0.0 all-gather.2.cloned.1.call-start
  7.2 2.8 fusion.10
  10.0 0.0 all-gather.2.cloned.1.call-update
  10.1 0.0 reduce-scatter.3.cloned.1.call-start
  10.1 0.9 exponential_multiply_fusion
  11.0 10.9 %fusion = (bf16[3328,1024]{1,0:T(8,128)(2,1)}, bf16[3328,1024]{1,0:T(8,128)(2,1)}) fusion(bf16[3328,1024]{1,0:T(8,128)(2,1)} %param.9, bf16[3328,1024]{1,0:T(8,128)(2,1)} %param.10, f32[26,1024]{1,0:T(8,128)S(1)} %exponential_multiply_fusion), kind=kLoop, calls=%fused_computation.2 | loop fusion | flops 23855104 | bytes 27369472 | tf_op jit(solution)/shard_map/convert_element_type | solution.py:29
  22.0 87.9 %all-gather.2.cloned.1.call-done = bf16[2048,3328]{1,0:T(8,128)(2,1)} async-done(((bf16[128,3328]{1,0:T(8,128)(2,1)}), bf16[2048,3328]{1,0:T(8,128)(2,1)}) %all-gather.2.cloned.1.call-update) | async-done | bytes 13631504 | tf_op jit(solution)/shard_map/all_gather | solution.py:24
  109.9 37.3 %fusion.2 = f32[2048,2048]{1,0:T(8,128)} fusion(bf16[2048,3328]{1,0:T(8,128)(2,1)} %all-gather.2.cloned.1.call-done, bf16[3328,1024]{1,0:T(8,128)(2,1)} %get-tuple-element.3, bf16[3328,1024]{1,0:T(8,128)(2,1)} %get-tuple-element.2), kind=kOutput, calls=%fused_computation.4 | convolution fusion | flops 27944550400 | bytes 44040192 | tf_op jit(solution)/shard_map/dot_general | solution.py:33
  147.2 0.0 copy-start
  147.2 0.0 reduce-scatter.3.cloned.1.call-update
  147.2 0.0 reduce-scatter.5.cloned.1.call-start
  147.2 145.2 %reduce-scatter.3.cloned.1.call-done = f32[512,2048]{1,0:T(8,128)} async-done(((f32[2048,2048]{1,0:T(8,128)}), f32[512,2048]{1,0:T(8,128)}) %reduce-scatter.3.cloned.1.call-update) | async-done | bytes 4194320 | tf_op jit(solution)/shard_map/reduce_scatter | solution.py:13
  292.4 0.0 reduce-scatter.5.cloned.1.call-update
  292.5 59.1 %reduce-scatter.5.cloned.1.call-done = f32[256,2048]{1,0:T(8,128)} async-done(((f32[512,2048]{1,0:T(8,128)}), f32[256,2048]{1,0:T(8,128)}) %reduce-scatter.5.cloned.1.call-update) | async-done | bytes 2097168 | tf_op jit(solution)/shard_map/reduce_scatter | solution.py:13
  351.6 0.0 copy-done
  351.6 2.8 fusion.12
Async XLA Ops:
  7.2 102.7 %all-gather.2.cloned.1.call-start = ((), (), s32[]{:S(2)}) async-start(), calls=%async_computation.2 | async-start | bytes 14483456 | tf_op jit(solution)/shard_map/all_gather | solution.py:24
  10.1 282.4 %reduce-scatter.3.cloned.1.call-start = ((), (), s32[]{:S(2)}) async-start(), calls=%async_computation.3 | async-start | bytes 20971520 | tf_op jit(solution)/shard_map/reduce_scatter | solution.py:13
  147.2 204.4 %copy-start = (bf16[256,1024]{1,0:T(8,128)(2,1)S(1)}, bf16[256,1024]{1,0:T(8,128)(2,1)}, u32[]{:S(2)}) copy-start(bf16[256,1024]{1,0:T(8,128)(2,1)} %param.8) | copy-start | bytes 1572868
  147.2 204.4 %reduce-scatter.5.cloned.1.call-start = ((), (), s32[]{:S(2)}) async-start(), calls=%async_computation.4 | async-start | bytes 6291456 | tf_op jit(solution)/shard_map/reduce_scatter | solution.py:13
Sparse Core Ops, SparseCore 0:
  10.4 99.4 all-gather.1
  147.3 145.0 reduce-scatter.2
  295.0 56.5 reduce-scatter.4
where the time goes:
time: 361 us
  waiting for transfers between devices  292 us (81%)
  matrix products  37.3 us (10%)
  other arithmetic  17.5 us (5%)
  between operations  13.7 us (4%)
    reduce_scatter x2, waiting for transfers between devices, own_rows(): so_far = lax.psum_scatter(so_far, axis, scatter_dimension=0, tiled=True)  204 us
    all_gather x1, waiting for transfers between devices, on_device(): hidden = lax.all_gather(swiglu(gate_pre, up_pre), 'col', axis=0, tiled=True)  87.9 us
    dot_general x1, matrix products, on_device(): jnp.dot(hidden, stacked, preferred_element_type=jnp.float32)  37.3 us
    convert_element_type x1, other arithmetic, on_device(): plus_weight = (weight_full + shift).astype(jnp.bfloat16)  10.9 us
  transfers between devices with their start and end apart: 3, of which 3 were waited for; matrix products, arithmetic and copies ran while one was open for 3% of the time, Pallas kernels for 0%

commit v1 on v0

--- a/solution.py
+++ b/solution.py
@@ -21,7 +21,10 @@
 
 
 def on_device(gate_pre, up_pre, residual, base_weight, perturb, exponents):
-    hidden = lax.all_gather(swiglu(gate_pre, up_pre), "col", axis=0, tiled=True)
+    hidden = jnp.concatenate(
+        lax.all_to_all(jnp.stack([swiglu(gate_pre, up_pre)] * lax.axis_size("col")), "col", 0, 0),
+        axis=0,
+    )
     group_size = base_weight.shape[0] // exponents.shape[0]
     factor = jnp.repeat(jnp.exp2(exponents.astype(jnp.float32)), group_size, axis=0)
     shift = step_size * factor * perturb.astype(jnp.float32)

time: 361 us -> 499 us (1.38)
  waiting for transfers between devices: 292 us -> 416 us
  starting transfers between devices: 0.12 us -> 9.51 us
  local copies, waits for them, and re-layouts: 0.01 us -> 6.19 us
    all_to_all x0 -> x1, waiting for transfers between devices: none -> 207 us  [on_device(): lax.all_to_all(jnp.stack([swiglu(gate_pre, up_pre)] * lax.axis_size('col'...]
    all_gather x1 -> x0, waiting for transfers between devices: 87.9 us -> none  [on_device(): hidden = lax.all_gather(swiglu(gate_pre, up_pre), 'col', axis=0, tiled=True)]
    all_to_all x0 -> x1, starting transfers between devices: none -> 9.43 us  [on_device(): lax.all_to_all(jnp.stack([swiglu(gate_pre, up_pre)] * lax.axis_size('col'...]
    another operation x0 -> x1, local copies, waits for them, and re-layouts: none -> 6.19 us  [on_device(): jnp.stack([swiglu(gate_pre, up_pre)] * lax.axis_size('col'))]
  transfers between devices with their start and end apart: 3 -> 3, of which waited for: 3 -> 3; matrix products, arithmetic and copies ran while one was open for 3% -> 2% of each run, Pallas kernels for 0% -> 0%
where the time goes in v1:
time: 499 us
  waiting for transfers between devices  416 us (83%)
  matrix products  37.3 us (7%)
  other arithmetic  15.7 us (3%)
  between operations  14.1 us (3%)
  starting transfers between devices  9.51 us (2%)
  local copies, waits for them, and re-layouts  6.19 us (1%)
    reduce_scatter x2, waiting for transfers between devices, own_rows(): so_far = lax.psum_scatter(so_far, axis, scatter_dimension=0, tiled=True)  209 us
    all_to_all x1, waiting for transfers between devices, on_device(): lax.all_to_all(jnp.stack([swiglu(gate_pre, up_pre)] * lax.axis_size('col'...  207 us
    dot_general x1, matrix products, on_device(): jnp.dot(hidden, stacked, preferred_element_type=jnp.float32)  37.3 us
    convert_element_type x1, other arithmetic, on_device(): plus_weight = (weight_full + shift).astype(jnp.bfloat16)  10.9 us
  transfers between devices with their start and end apart: 3, of which 3 were waited for; matrix products, arithmetic and copies ran while one was open for 2% of the time, Pallas kernels for 0%

profile of v1, /device:TPU:1, one launch (start us, length us, event | category | flops | bytes accessed | tf_op | source)
XLA Modules:
  0.0 499.1 jit_solution(5914977842809859964)
XLA Ops:
  7.2 1.9 fusion.10
  9.1 6.2 %stack.2 = bf16[16,128,3328]{2,1,0:T(8,128)(2,1)} broadcast(bf16[128,3328]{1,0:T(8,128)(2,1)S(1)} %fusion.10), dimensions={1,2} | broadcast | bytes 14483456 | tf_op jit(solution)/shard_map/stack | solution.py:25
  15.3 0.0 copy-start.1
  15.3 9.4 %all-to-all-start = ((bf16[16,128,3328]{2,1,0:T(8,128)(2,1)}), bf16[16,128,3328]{2,1,0:T(8,128)(2,1)}, u32[]{:S(2)}, u32[]{:S(2)}) async-start(bf16[16,128,3328]{2,1,0:T(8,128)(2,1)} %stack.2), calls=%async_computation | async-start | bytes 27262976 | tf_op jit(solution)/shard_map/all_to_all | solution.py:25
  24.7 0.0 reduce-scatter.3.cloned.1.call-start
  24.8 0.0 copy-done.1
  24.8 10.9 %fusion = (bf16[3328,1024]{1,0:T(8,128)(2,1)}, bf16[3328,1024]{1,0:T(8,128)(2,1)}) fusion(bf16[3328,1024]{1,0:T(8,128)(2,1)} %param.9, bf16[3328,1024]{1,0:T(8,128)(2,1)} %param.10, f32[26,1024]{1,0:T(8,128)S(1)} %exponential_multiply_fusion), kind=kLoop, calls=%fused_computation.2 | loop fusion | flops 23855104 | bytes 27369472 | tf_op jit(solution)/shard_map/convert_element_type | solution.py:32
  35.7 207.0 %all-to-all-done = bf16[16,128,3328]{2,1,0:T(8,128)(2,1)} async-done(((bf16[16,128,3328]{2,1,0:T(8,128)(2,1)}), bf16[16,128,3328]{2,1,0:T(8,128)(2,1)}, u32[]{:S(2)}, u32[]{:S(2)}) %all-to-all-start) | async-done | bytes 13631520 | tf_op jit(solution)/shard_map/all_to_all | solution.py:25
  242.8 37.3 %fusion.2 = f32[2048,2048]{1,0:T(8,128)} fusion(bf16[2048,3328]{1,0:T(8,128)(2,1)} %bitcast, bf16[3328,1024]{1,0:T(8,128)(2,1)} %get-tuple-element.3, bf16[3328,1024]{1,0:T(8,128)(2,1)} %get-tuple-element.2), kind=kOutput, calls=%fused_computation.4 | convolution fusion | flops 27944550400 | bytes 44040192 | tf_op jit(solution)/shard_map/dot_general | solution.py:36
  280.0 0.0 copy-start
  280.0 0.0 reduce-scatter.3.cloned.1.call-update
  280.0 0.0 reduce-scatter.5.cloned.1.call-start
  280.1 150.1 %reduce-scatter.3.cloned.1.call-done = f32[512,2048]{1,0:T(8,128)} async-done(((f32[2048,2048]{1,0:T(8,128)}), f32[512,2048]{1,0:T(8,128)}) %reduce-scatter.3.cloned.1.call-update) | async-done | bytes 4194320 | tf_op jit(solution)/shard_map/reduce_scatter | solution.py:13
  430.2 0.0 reduce-scatter.5.cloned.1.call-update
  430.2 59.1 %reduce-scatter.5.cloned.1.call-done = f32[256,2048]{1,0:T(8,128)} async-done(((f32[512,2048]{1,0:T(8,128)}), f32[256,2048]{1,0:T(8,128)}) %reduce-scatter.5.cloned.1.call-update) | async-done | bytes 2097168 | tf_op jit(solution)/shard_map/reduce_scatter | solution.py:13
  489.4 0.0 copy-done
  489.4 2.8 fusion.12
  (1 shorter events, 0.0 us)
Async XLA Ops:
  15.3 9.5 %copy-start.1 = (s32[26,1024]{1,0:T(8,128)S(1)}, s32[26,1024]{1,0:T(8,128)}, u32[]{:S(2)}) copy-start(s32[26,1024]{1,0:T(8,128)} %param.11) | copy-start | bytes 319492
  15.3 227.5 %all-to-all-start = ((bf16[16,128,3328]{2,1,0:T(8,128)(2,1)}), bf16[16,128,3328]{2,1,0:T(8,128)(2,1)}, u32[]{:S(2)}, u32[]{:S(2)}) async-start(bf16[16,128,3328]{2,1,0:T(8,128)(2,1)} %stack.2), calls=%async_computation | async-start | bytes 27262976 | tf_op jit(solution)/shard_map/all_to_all | solution.py:25
  24.7 405.5 %reduce-scatter.3.cloned.1.call-start = ((), (), s32[]{:S(2)}) async-start(), calls=%async_computation.3 | async-start | bytes 20971520 | tf_op jit(solution)/shard_map/reduce_scatter | solution.py:13
  280.0 209.4 %copy-start = (bf16[256,1024]{1,0:T(8,128)(2,1)S(1)}, bf16[256,1024]{1,0:T(8,128)(2,1)}, u32[]{:S(2)}) copy-start(bf16[256,1024]{1,0:T(8,128)(2,1)} %param.8) | copy-start | bytes 1572868
  280.0 209.3 %reduce-scatter.5.cloned.1.call-start = ((), (), s32[]{:S(2)}) async-start(), calls=%async_computation.4 | async-start | bytes 6291456 | tf_op jit(solution)/shard_map/reduce_scatter | solution.py:13
Sparse Core Ops, SparseCore 0:
  280.2 150.0 reduce-scatter.2
  432.7 56.5 reduce-scatter.4
